TPU v7x, 32 devices: a whole 2x2x4 slice. The times are simulated.
32 devices in a mesh: rep: 1, seq: 16 (over z, y, core), head: 2 (over x).
Axes of the slice: x: 2, y: 2, z: 4, core: 2. Of those that a mesh axis runs over, the one named last changes fastest.
Arguments:
- states: bfloat16 [256, 8192], P('rep', 'seq'), may hold values from -6 to 6
- w_query: bfloat16 [8192, 8192], P('seq', 'head'), may hold values from -0.0625 to 0.0625
- w_key: bfloat16 [8192, 1024], P('seq', 'head'), may hold values from -0.3125 to 0.3125
- w_value: bfloat16 [8192, 1024], P('seq', 'head'), may hold values from -0.25 to 0.25
- w_out: bfloat16 [8192, 8192], P('head', 'seq'), may hold values from -0.09375 to 0.09375
- key_cache: bfloat16 [2, 8192, 1024], P('rep', 'seq', 'head'), may hold values from -480 to 480
- value_cache: bfloat16 [2, 8192, 1024], P('rep', 'seq', 'head'), may hold values from -24 to 24
- parents: int32 [2, 128], P('rep'), may hold values from 0 to 126, as said below
- cache_lengths: int32 [2], P('rep'), may hold values from 2048 to 8192, as said below
Outputs:
- attended: bfloat16 [256, 8192], P('rep', ('seq', 'head'))
Inputs may be any that keep to these rules, and one draw needn't show every extreme that they name: parents[t, 0] = 0, parents[t, i] < i for i >= 1, and the last node's parent is node 126. `cache_lengths`: at least one sequence fills all 8192 positions.
All inputs are finite; a program needn't handle non-finite values.
Results may differ from a plain program's by a relative error of at most 0.014.
The roundings to bfloat16 on the way count: a program that leaves them out, or rounds other values in their place, can miss the bound.
Values may be sent and summed in bfloat16 or wider, within the bound.
No kernel may reach another device: no remote copies, remote signals or barrier semaphores. Data moves between devices by JAX's collectives and lax.ppermute only.
A program may use at most 320 MiB of HBM per device.

v0:
```python
import jax
import jax.numpy as jnp
from jax import lax
from jax.sharding import PartitionSpec as P

HEAD_DIM = 128
rope_base = 500000.0
neg_big = -1e30


def ancestry(parents):
    count = parents.shape[1]
    ident = jnp.eye(count, dtype=jnp.float32)
    onehot = (parents[:, :, None] == jnp.arange(count, dtype=jnp.int32)[None, None, :]).astype(
        jnp.float32
    )
    reach = jnp.minimum(ident[None] + onehot, 1.0)
    for level in range(max(1, (count - 1).bit_length())):
        reach = jnp.minimum(
            jnp.einsum("tij,tjk->tik", reach, reach, precision=lax.Precision.HIGHEST), 1.0
        )
    return reach


def rotate(values, position):
    count = values.shape[0]
    half = HEAD_DIM // 2
    shaped = values.reshape(count, -1, HEAD_DIM)
    freq = rope_base ** (-(jnp.arange(half, dtype=jnp.float32) * 2.0 / HEAD_DIM))
    angle = position[:, None] * freq[None, :]
    cosine = jnp.cos(angle)[:, None, :]
    sine = jnp.sin(angle)[:, None, :]
    first = shaped[..., :half]
    second = shaped[..., half:]
    turned = jnp.concatenate([first * cosine - second * sine, second * cosine + first * sine], -1)
    return turned.reshape(count, -1)


def combine(left, right):
    top = jnp.maximum(left[0], right[0])
    scale_left = jnp.exp(left[0] - top)
    scale_right = jnp.exp(right[0] - top)
    return (
        top,
        left[1] * scale_left + right[1] * scale_right,
        left[2] * scale_left[..., None] + right[2] * scale_right[..., None],
    )


def cache_state(query, keys, values, length, offset):
    total = keys.shape[0]
    block = min(total, 2048)
    count = total // block
    rows_here, kv_local, group, width = query.shape
    scale = width ** (-0.5)
    keys = keys.reshape(count, block, kv_local, width)
    values = values.reshape(count, block, kv_local, width)

    def step(carry, inputs):
        key_block, value_block, first = inputs
        valid = offset + first + jnp.arange(block, dtype=jnp.int32) < length
        scores = (
            jnp.einsum("rkgd,nkd->rkgn", query, key_block, preferred_element_type=jnp.float32)
            * scale
        )
        scores = jnp.where(valid, scores, neg_big)
        top = jnp.maximum(carry[0], jnp.max(scores, -1))
        weights = jnp.where(valid, jnp.exp(scores - top[..., None]), 0.0)
        shrink = jnp.exp(carry[0] - top)
        mass = carry[1] * shrink + jnp.sum(weights, -1)
        acc = carry[2] * shrink[..., None] + jnp.einsum(
            "rkgn,nkd->rkgd",
            weights.astype(jnp.bfloat16),
            value_block,
            preferred_element_type=jnp.float32,
        )
        return ((top, mass, acc), None)

    init = (
        jnp.full((rows_here, kv_local, group), neg_big, jnp.float32),
        jnp.zeros((rows_here, kv_local, group), jnp.float32),
        jnp.zeros((rows_here, kv_local, group, width), jnp.float32),
    )
    firsts = jnp.arange(count, dtype=jnp.int32) * block
    state, _ = lax.scan(step, init, (keys, values, firsts))
    return state


def tree_state(query, new_keys, new_values, allowed):
    rows_here, kv_local, group, width = query.shape
    scale = width ** (-0.5)
    keys = new_keys.reshape(-1, kv_local, width)
    values = new_values.reshape(-1, kv_local, width)
    mask = allowed[:, None, None, :]
    scores = jnp.einsum("rkgd,nkd->rkgn", query, keys, preferred_element_type=jnp.float32) * scale
    scores = jnp.where(mask, scores, neg_big)
    top = jnp.max(scores, -1)
    weights = jnp.where(mask, jnp.exp(scores - top[..., None]), 0.0)
    acc = jnp.einsum(
        "rkgn,nkd->rkgd", weights.astype(jnp.bfloat16), values, preferred_element_type=jnp.float32
    )
    return (top, jnp.sum(weights, -1), acc)


def local(states, w_query, w_key, w_value, w_out, key_cache, value_cache, parents, cache_lengths):
    trees, tree_rows = parents.shape
    rows = trees * tree_rows
    kv_local = key_cache.shape[2] // HEAD_DIM
    heads_local = w_query.shape[1] // HEAD_DIM
    group = heads_local // kv_local
    reach = ancestry(parents)
    position = (cache_lengths.astype(jnp.float32)[:, None] + jnp.sum(reach, -1) - 1.0).reshape(-1)
    allowed = (jnp.eye(trees, dtype=jnp.float32)[:, None, :, None] * reach[:, :, None, :]).reshape(
        rows, rows
    ) > 0.5
    q_part = jnp.dot(states, w_query, preferred_element_type=jnp.float32)
    k_part = jnp.dot(states, w_key, preferred_element_type=jnp.float32)
    v_part = jnp.dot(states, w_value, preferred_element_type=jnp.float32)
    q_raw, k_raw, v_raw = lax.psum((q_part, k_part, v_part), "seq")
    queries = rotate(q_raw, position).astype(jnp.bfloat16)
    new_keys = rotate(k_raw, position).astype(jnp.bfloat16)
    new_values = v_raw.astype(jnp.bfloat16)
    query_heads = queries.reshape(rows, kv_local, group, HEAD_DIM)
    offset = lax.axis_index("seq") * key_cache.shape[1]
    parts_list = []
    for tree in range(trees):
        parts_list.append(
            cache_state(
                query_heads[tree * tree_rows : (tree + 1) * tree_rows],
                key_cache[tree],
                value_cache[tree],
                cache_lengths[tree],
                offset,
            )
        )
    peak = jnp.concatenate([item[0] for item in parts_list], 0)
    mass = jnp.concatenate([item[1] for item in parts_list], 0)
    acc = jnp.concatenate([item[2] for item in parts_list], 0)
    summit = lax.pmax(peak, "seq")
    factor = jnp.exp(peak - summit)
    mass_share, acc_share = (
        lax.psum_scatter(mass * factor, "seq", scatter_dimension=0, tiled=True),
        lax.psum_scatter(acc * factor[..., None], "seq", scatter_dimension=0, tiled=True),
    )
    share = mass_share.shape[0]
    first_row = lax.axis_index("seq") * share
    summit_share = lax.dynamic_slice_in_dim(summit, first_row, share)
    query_share = lax.dynamic_slice_in_dim(query_heads, first_row, share)
    allowed_share = lax.dynamic_slice_in_dim(allowed, first_row, share)
    total = combine(
        (summit_share, mass_share, acc_share),
        tree_state(query_share, new_keys, new_values, allowed_share),
    )
    attention_share = (total[2] / total[1][..., None]).reshape(share, -1).astype(jnp.bfloat16)
    attention = lax.all_gather(attention_share, "seq", axis=0, tiled=True)
    partial_value = jnp.dot(attention, w_out, preferred_element_type=jnp.float32)
    return lax.psum_scatter(partial_value, "head", scatter_dimension=1, tiled=True).astype(
        jnp.bfloat16
    )


def solution(mesh):
    placed = (
        P("rep", "seq"),
        P("seq", "head"),
        P("seq", "head"),
        P("seq", "head"),
        P("head", "seq"),
        P("rep", "seq", "head"),
        P("rep", "seq", "head"),
        P("rep", None),
        P("rep"),
    )
    return jax.shard_map(
        local, mesh=mesh, in_specs=placed, out_specs=P("rep", ("seq", "head")), check_vma=False
    )
```

profile of v0, /device:TPU:0, one launch (start us, length us, event | category | flops | bytes accessed | tf_op | source)
XLA Modules:
  0.0 412.9 jit_solution(16273453118756324011)
XLA Ops:
  6.5 1.0 copy-done
  7.6 1.2 convolution_bitcast_fusion.1
  8.8 0.9 copy.84
  9.7 3.5 convolution_bitcast_fusion
  13.2 2.7 copy.76
  16.0 1.1 copy-done.6
  18.0 1.0 copy.74
  19.2 1.0 copy.72
  20.4 1.8 fusion.47
  25.0 110.8 %all-reduce.4.cloned.1.call-done = (f32[256,4,128]{2,0,1:T(8,128)}, f32[256,32,128]{2,1,0:T(8,128)}) async-done(((f32[256,4,128]{2,0,1:T(8,128)}, f32[256,32,128]{2,1,0:T(8,128)}), (f32[256,4,128]{2,0,1:T(8,128)}, f32[256,32,128]{2,1,0:T(8,128)})) %all-reduce.4.cloned.1.call-update) | async-done | bytes 4718608 | tf_op jit(solution)/shard_map/psum | solution.py:119
  135.7 4.8 %multiply_subtract_fusion = (bf16[256,32,64]{2,1,0:T(8,128)(2,1)S(1)}, bf16[256,32,64]{2,1,0:T(8,128)(2,1)S(1)}) fusion(f32[256,32,128]{2,1,0:T(8,128)} %get-tuple-element.40, f32[256,64]{1,0:T(8,128)S(1)} %get-tuple-element.81, f32[256,64]{1,0:T(8,128)S(1)} %get-tuple-element.80), kind=kLoop, calls=%fused_computation.17 | loop fusion | flops 4194304 | bytes 6422528 | tf_op jit(solution)/shard_map/sub | solution.py:35
  140.6 1.2 maximum_convert_fusion
  142.5 1.3 bitcast_reduce_fusion
  143.9 3.1 fusion.6
  148.1 1.3 bitcast_reduce_fusion.1
  149.5 2.4 fusion.4
  151.9 0.8 copy-done.3
  153.3 60.0 %pmax.7 = f32[256,4,8]{0,2,1:T(8,128)S(1)} all-reduce(f32[256,4,8]{0,2,1:T(8,128)S(1)} %pad_maximum_fusion), channel_id=1, replica_groups=mesh['rep'=1,'seq'=16,'head'=2] {'seq'}, use_global_device_ids=true, to_apply=%region_4.5 | all-reduce | flops 8192 | bytes 65536 | tf_op jit(solution)/shard_map/pmax | solution.py:139
  215.0 5.7 %bitcast_add_fusion = f32[128,4,8,128]{3,0,2,1:T(8,128)S(1)} fusion(bf16[512,4,128,1]{0,2,3,1:T(8,128)(2,1)S(1)} %bitcast.140, f32[4,128,8,512]{3,1,2,0:T(8,128)} %copy-done.2, f32[128,4,8]{0,2,1:T(8,128)S(1)} %broadcast_maximum_fusion, pred[512]{0:T(512)(128)(4,1)} %copy-done.19, f32[128,4,8]{0,2,1:T(8,128)} %get-tuple-element.79), kind=kOutput, calls=%fused_computation.25 | convolution fusion | flops 547880960 | bytes 11043328 | tf_op jit(solution)/shard_map/while/body/eval_jaxpr/rkgn,nkd->rkgd/dot_general | solution.py:71
  220.7 5.5 %bitcast_add_fusion.1 = f32[128,4,8,128]{3,0,2,1:T(8,128)S(1)} fusion(bf16[512,4,128,1]{0,2,3,1:T(8,128)(2,1)S(1)} %bitcast.139, f32[4,128,8,512]{3,1,2,0:T(8,128)} %copy-done.3, f32[128,4,8]{0,2,1:T(8,128)S(1)} %copy-done.11, pred[512]{0:T(512)(128)(4,1)S(1)} %copy-done.18, f32[128,4,8]{0,2,1:T(8,128)S(1)} %copy-done.16), kind=kOutput, calls=%fused_computation.26 | convolution fusion | flops 547880960 | bytes 11043328 | tf_op jit(solution)/shard_map/while/body/eval_jaxpr/rkgn,nkd->rkgd/dot_general | solution.py:71
  226.2 2.6 maximum_multiply_fusion
  229.8 2.1 fusion.69
  231.9 63.7 %all-reduce.5 = bf16[256,512]{1,0:T(8,128)(2,1)S(1)} all-reduce(f32[256,512]{1,0:T(8,128)} %fusion.69), channel_id=1, replica_groups=mesh['rep'=1,'seq'=16,'head'=2] {'seq'}, use_global_device_ids=true, to_apply=%region_8.9 | all-reduce | flops 131072 | bytes 786432 | tf_op jit(solution)/shard_map/psum | solution.py:119
  295.6 0.8 reshape.143
  296.4 0.8 copy.46
  298.2 0.8 copy.70
  299.1 44.5 %reduce-scatter.6.cloned.1.call-done = f32[16,4,8,128]{3,0,2,1:T(8,128)} async-done(((f32[256,4,8,128]{3,0,2,1:T(8,128)}), f32[16,4,8,128]{3,0,2,1:T(8,128)}) %reduce-scatter.6.cloned.1.call-update) | async-done | bytes 262160 | tf_op jit(solution)/shard_map/reduce_scatter | solution.py:143
  343.5 1.4 fusion.25
  345.7 40.6 %all-gather.2.cloned.1.call-done = bf16[256,4096]{1,0:T(8,128)(2,1)} async-done(((bf16[16,4096]{1,0:T(8,128)(2,1)}), bf16[256,4096]{1,0:T(8,128)(2,1)}) %all-gather.2.cloned.1.call-update) | async-done | bytes 2097168 | tf_op jit(solution)/shard_map/all_gather | solution.py:155
  386.4 4.9 %fusion.70 = f32[256,512]{1,0:T(8,128)} fusion(bf16[256,4096]{1,0:T(8,128)(2,1)} %all-gather.2.cloned.1.call-done, bf16[4096,512]{1,0:T(8,128)(2,1)} %param.13), kind=kOutput, calls=%fused_computation.111 | convolution fusion | flops 1073741824 | bytes 6815744 | tf_op jit(solution)/shard_map/dot_general | solution.py:156
  391.3 13.5 %reduce-scatter.8.cloned.1.call-done = f32[256,256]{1,0:T(8,128)} async-done(((f32[256,512]{1,0:T(8,128)}), f32[256,256]{1,0:T(8,128)}) %reduce-scatter.8.cloned.1.call-update) | async-done | bytes 262160 | tf_op jit(solution)/shard_map/reduce_scatter | solution.py:157
  404.8 1.6 convert_element_type.65
  (89 shorter events, 10.9 us)
Async XLA Ops:
  6.5 1.0 copy-start
  6.5 129.2 %all-reduce.4.cloned.1.call-start = ((), (), s32[]{:S(2)}) async-start(), calls=%async_computation.7 | async-start | bytes 9437184 | tf_op jit(solution)/shard_map/psum | solution.py:119
  16.0 1.2 copy-start.6
  16.0 1.3 copy-start.20
  16.0 1.9 copy-start.7
  16.0 6.2 %copy-start.21 = (s32[2,128]{1,0:T(2,128)S(1)}, s32[2,128]{1,0:T(2,128)}, u32[]{:S(2)}) copy-start(s32[2,128]{1,0:T(2,128)} %param.16) | copy-start | bytes 3076
  16.0 282.2 %reduce-scatter.10.cloned.1.call-start = ((), (), s32[]{:S(2)}) async-start(), calls=%async_computation.6 | async-start | bytes 139264
  22.2 120.3 %copy-start.19 = (pred[512]{0:T(512)(128)(4,1)}, pred[512]{0:T(512)(128)(4,1)S(1)}, u32[]{:S(2)}) copy-start(pred[512]{0:T(512)(128)(4,1)S(1)} %get-tuple-element.92) | copy-start | bytes 1540
  143.9 3.2 copy-start.2
  143.9 4.3 %copy-start.17 = (pred[512]{0:T(512)(128)(4,1)S(1)}, pred[512]{0:T(512)(128)(4,1)}, u32[]{:S(2)}) copy-start(pred[512]{0:T(512)(128)(4,1)} %get-tuple-element.93) | copy-start | bytes 1540
  149.5 3.2 copy-start.3
  149.5 63.8 %copy-start.10 = (f32[128,4,8]{0,2,1:T(8,128)}, f32[128,4,8]{0,2,1:T(8,128)S(1)}, u32[]{:S(2)}) copy-start(f32[128,4,8]{0,2,1:T(8,128)S(1)} %broadcast_maximum_fusion.1) | copy-start | bytes 49156
  149.5 63.8 %copy-start.15 = (f32[128,4,8]{0,2,1:T(8,128)S(1)}, f32[128,4,8]{0,2,1:T(8,128)}, u32[]{:S(2)}) copy-start(f32[128,4,8]{0,2,1:T(8,128)} %get-tuple-element.78) | copy-start | bytes 49156
  149.5 65.4 %copy-start.9 = (bf16[1,512,512]{1,2,0:T(8,128)(2,1)S(1)}, bf16[1,512,512]{1,2,0:T(8,128)(2,1)}, u32[]{:S(2)}) copy-start(bf16[1,512,512]{1,2,0:T(8,128)(2,1)} %copy.74) | copy-start | bytes 1572868
  213.3 1.6 copy-start.12
  214.7 128.8 %reduce-scatter.6.cloned.1.call-start = ((), (), s32[]{:S(2)}) async-start(), calls=%async_computation.3 | async-start | bytes 4456448 | tf_op jit(solution)/shard_map/reduce_scatter | solution.py:143
  214.9 5.7 %copy-start.8 = (bf16[1,512,512]{1,2,0:T(8,128)(2,1)S(1)}, bf16[1,512,512]{1,2,0:T(8,128)(2,1)}, u32[]{:S(2)}) copy-start(bf16[1,512,512]{1,2,0:T(8,128)(2,1)} %copy.72) | copy-start | bytes 1572868
  215.0 5.7 %copy-start.11 = (f32[128,4,8]{0,2,1:T(8,128)S(1)}, f32[128,4,8]{0,2,1:T(8,128)}, u32[]{:S(2)}) copy-start(f32[128,4,8]{0,2,1:T(8,128)} %copy-done.10) | copy-start | bytes 49156
  215.0 5.7 %copy-start.16 = (f32[128,4,8]{0,2,1:T(8,128)S(1)}, f32[128,4,8]{0,2,1:T(8,128)}, u32[]{:S(2)}) copy-start(f32[128,4,8]{0,2,1:T(8,128)} %get-tuple-element.77) | copy-start | bytes 49156
  215.0 5.7 %copy-start.18 = (pred[512]{0:T(512)(128)(4,1)S(1)}, pred[512]{0:T(512)(128)(4,1)}, u32[]{:S(2)}) copy-start(pred[512]{0:T(512)(128)(4,1)} %get-tuple-element.93) | copy-start | bytes 1540
  220.7 5.5 %copy-start.14 = (f32[256,4,8]{0,2,1:T(8,128)S(1)}, f32[256,4,8]{0,2,1:T(8,128)}, u32[]{:S(2)}) copy-start(f32[256,4,8]{0,2,1:T(8,128)} %get-tuple-element.54) | copy-start | bytes 98308
  228.8 1.0 copy-start.4
  228.8 68.4 %copy-start.5 = (f32[256,4,128]{2,0,1:T(8,128)S(1)}, f32[256,4,128]{2,0,1:T(8,128)}, u32[]{:S(2)}) copy-start(f32[256,4,128]{2,0,1:T(8,128)} %get-tuple-element.39) | copy-start | bytes 1572868
  228.8 157.5 %all-gather.2.cloned.1.call-start = ((), (), s32[]{:S(2)}) async-start(), calls=%async_computation.4 | async-start | bytes 2228224 | tf_op jit(solution)/shard_map/all_gather | solution.py:155
  295.6 3.3 copy-start.13
  345.7 60.7 %copy-start.1 = (bf16[512,512]{1,0:T(8,128)(2,1)S(1)}, bf16[512,512]{1,0:T(8,128)(2,1)}, u32[]{:S(2)}) copy-start(bf16[512,512]{1,0:T(8,128)(2,1)} %param.11) | copy-start | bytes 1572868
  345.7 59.1 %reduce-scatter.8.cloned.1.call-start = ((), (), s32[]{:S(2)}) async-start(), calls=%async_computation.5 | async-start | bytes 786432 | tf_op jit(solution)/shard_map/reduce_scatter | solution.py:157
Sparse Core Ops, SparseCore 0:
  16.1 119.5 all-reduce.3
  214.8 52.9 reduce-scatter.9
  271.7 71.8 reduce-scatter.5
  345.8 40.5 all-gather.1
  391.4 13.3 reduce-scatter.7
where the time goes:
time: 414 us; the launch traced here: 413 us
  waiting for transfers between devices  209 us (50%)
  blocking collectives  124 us (30%)
  matrix products  29.4 us (7%)
  other arithmetic  20.9 us (5%)
  local copies, waits for them, and re-layouts  15.5 us (4%)
  between operations  13.6 us (3%)
    psum x1, waiting for transfers between devices, local(): q_raw, k_raw, v_raw = lax.psum((q_part, k_part, v_part), 'seq')  111 us
    psum x1, blocking collectives, local(): q_raw, k_raw, v_raw = lax.psum((q_part, k_part, v_part), 'seq')  63.7 us
    pmax x1, blocking collectives, local(): summit = lax.pmax(peak, 'seq')  60 us
    reduce_scatter x1, waiting for transfers between devices, local(): lax.psum_scatter(acc * factor[..., None], 'seq', scatter_dimension=0, til...  44.5 us
    all_gather x1, waiting for transfers between devices, local(): attention = lax.all_gather(attention_share, 'seq', axis=0, tiled=True)  40.6 us
    reduce_scatter x1, waiting for transfers between devices, local(): lax.psum_scatter(partial_value, 'head', scatter_dimension=1, tiled=True)  13.5 us
    unnamed x53, local copies, waits for them, and re-layouts  11.1 us
    dot_general x2, matrix products, step(): jnp.einsum('rkgn,nkd->rkgd', weights.astype(jnp.bfloat16), value_block, p...  11.1 us
  transfers between devices with their start and end apart: 5, of which 4 were waited for; matrix products, arithmetic and copies ran while one was open for 7% of the time, Pallas kernels for 0%

commit v1 on v0

--- a/solution.py
+++ b/solution.py
@@ -152,7 +152,18 @@
         tree_state(query_share, new_keys, new_values, allowed_share),
     )
     attention_share = (total[2] / total[1][..., None]).reshape(share, -1).astype(jnp.bfloat16)
-    attention = lax.all_gather(attention_share, "seq", axis=0, tiled=True)
+    many = lax.axis_size("seq")
+    all_blocks = []
+    for m in range(1, many):
+        all_blocks.append((m - 1, m))
+    far_arr = all_blocks + [(many - 1, 0)]
+    a_now = attention_share
+    blocks_here = [a_now]
+    for _ in range(many - 1):
+        a_now = lax.ppermute(a_now, "seq", far_arr)
+        blocks_here += [a_now]
+    clean = jnp.concatenate([*reversed(blocks_here)], 0)
+    attention = jnp.roll(clean, (lax.axis_index("seq") + 1) * a_now.shape[0], 0)
     partial_value = jnp.dot(attention, w_out, preferred_element_type=jnp.float32)
     return lax.psum_scatter(partial_value, "head", scatter_dimension=1, tiled=True).astype(
         jnp.bfloat16

time: 414 us -> 475 us (1.15)
  waiting for transfers between devices: 209 us -> 273 us
    ppermute x0 -> x15, waiting for transfers between devices: none -> 106 us  [local(): a_now = lax.ppermute(a_now, 'seq', far_arr)]
    all_gather x1 -> x0, waiting for transfers between devices: 40.6 us -> none  [local(): attention = lax.all_gather(attention_share, 'seq', axis=0, tiled=True)]
    unnamed x53 -> x86, local copies, waits for them, and re-layouts: 11.1 us -> 11 us
  transfers between devices with their start and end apart: 5 -> 19, of which waited for: 4 -> 18; matrix products, arithmetic and copies ran while one was open for 7% -> 6% of each run, Pallas kernels for 0% -> 0%
where the time goes in v1:
time: 475 us; the launch traced here: 474 us
  waiting for transfers between devices  273 us (57%)
  blocking collectives  124 us (26%)
  matrix products  26.6 us (6%)
  other arithmetic  20.8 us (4%)
  local copies, waits for them, and re-layouts  15.5 us (3%)
  between operations  13.9 us (3%)
    psum x1, waiting for transfers between devices, local(): q_raw, k_raw, v_raw = lax.psum((q_part, k_part, v_part), 'seq')  111 us
    ppermute x15, waiting for transfers between devices, local(): a_now = lax.ppermute(a_now, 'seq', far_arr)  106 us
    psum x1, blocking collectives, local(): q_raw, k_raw, v_raw = lax.psum((q_part, k_part, v_part), 'seq')  63.8 us
    pmax x1, blocking collectives, local(): summit = lax.pmax(peak, 'seq')  60 us
    reduce_scatter x1, waiting for transfers between devices, local(): lax.psum_scatter(acc * factor[..., None], 'seq', scatter_dimension=0, til...  44.3 us
    reduce_scatter x1, waiting for transfers between devices, local(): lax.psum_scatter(partial_value, 'head', scatter_dimension=1, tiled=True)  12 us
    dot_general x2, matrix products, step(): jnp.einsum('rkgn,nkd->rkgd', weights.astype(jnp.bfloat16), value_block, p...  11.2 us
    unnamed x86, local copies, waits for them, and re-layouts  11 us
  transfers between devices with their start and end apart: 19, of which 18 were waited for; matrix products, arithmetic and copies ran while one was open for 6% of the time, Pallas kernels for 0%

profile of v1, /device:TPU:0, one launch (start us, length us, event | category | flops | bytes accessed | tf_op | source)
XLA Modules:
  0.0 474.5 jit_solution(10311876408813483553)
XLA Ops:
  9.7 3.5 convolution_bitcast_fusion
  13.3 2.8 copy.76
  20.5 1.8 fusion.49
  25.1 110.8 %all-reduce.4.cloned.1.call-done = (f32[256,4,128]{2,0,1:T(8,128)}, f32[256,32,128]{2,1,0:T(8,128)}) async-done(((f32[256,4,128]{2,0,1:T(8,128)}, f32[256,32,128]{2,1,0:T(8,128)}), (f32[256,4,128]{2,0,1:T(8,128)}, f32[256,32,128]{2,1,0:T(8,128)})) %all-reduce.4.cloned.1.call-update) | async-done | bytes 4718608 | tf_op jit(solution)/shard_map/psum | solution.py:119
  135.8 4.8 %multiply_subtract_fusion = (bf16[256,32,64]{2,1,0:T(8,128)(2,1)S(1)}, bf16[256,32,64]{2,1,0:T(8,128)(2,1)S(1)}) fusion(f32[256,32,128]{2,1,0:T(8,128)} %get-tuple-element.40, f32[256,64]{1,0:T(8,128)S(1)} %get-tuple-element.81, f32[256,64]{1,0:T(8,128)S(1)} %get-tuple-element.80), kind=kLoop, calls=%fused_computation.17 | loop fusion | flops 4194304 | bytes 6422528 | tf_op jit(solution)/shard_map/sub | solution.py:35
  144.0 3.0 fusion.6
  149.6 2.4 fusion.4
  153.4 60.0 %pmax.7 = f32[256,4,8]{0,2,1:T(8,128)S(1)} all-reduce(f32[256,4,8]{0,2,1:T(8,128)S(1)} %pad_maximum_fusion), channel_id=1, replica_groups=mesh['rep'=1,'seq'=16,'head'=2] {'seq'}, use_global_device_ids=true, to_apply=%region_4.5 | all-reduce | flops 8192 | bytes 65536 | tf_op jit(solution)/shard_map/pmax | solution.py:139
  215.1 5.7 %bitcast_add_fusion = f32[128,4,8,128]{3,0,2,1:T(8,128)S(1)} fusion(bf16[512,4,128,1]{0,2,3,1:T(8,128)(2,1)S(1)} %bitcast.146, f32[4,128,8,512]{3,1,2,0:T(8,128)} %copy-done.2, f32[128,4,8]{0,2,1:T(8,128)S(1)} %broadcast_maximum_fusion, pred[512]{0:T(512)(128)(4,1)} %copy-done.19, f32[128,4,8]{0,2,1:T(8,128)} %get-tuple-element.79), kind=kOutput, calls=%fused_computation.25 | convolution fusion | flops 547880960 | bytes 11043328 | tf_op jit(solution)/shard_map/while/body/eval_jaxpr/rkgn,nkd->rkgd/dot_general | solution.py:71
  220.9 5.5 %bitcast_add_fusion.1 = f32[128,4,8,128]{3,0,2,1:T(8,128)S(1)} fusion(bf16[512,4,128,1]{0,2,3,1:T(8,128)(2,1)S(1)} %bitcast.145, f32[4,128,8,512]{3,1,2,0:T(8,128)} %copy-done.3, f32[128,4,8]{0,2,1:T(8,128)S(1)} %copy-done.11, pred[512]{0:T(512)(128)(4,1)S(1)} %copy-done.18, f32[128,4,8]{0,2,1:T(8,128)S(1)} %copy-done.16), kind=kOutput, calls=%fused_computation.26 | convolution fusion | flops 547880960 | bytes 11043328 | tf_op jit(solution)/shard_map/while/body/eval_jaxpr/rkgn,nkd->rkgd/dot_general | solution.py:71
  226.4 2.6 maximum_multiply_fusion
  229.9 2.2 fusion.72
  232.1 63.8 %all-reduce.5 = bf16[256,512]{1,0:T(8,128)(2,1)S(1)} all-reduce(f32[256,512]{1,0:T(8,128)} %fusion.72), channel_id=1, replica_groups=mesh['rep'=1,'seq'=16,'head'=2] {'seq'}, use_global_device_ids=true, to_apply=%region_8.9 | all-reduce | flops 131072 | bytes 786432 | tf_op jit(solution)/shard_map/psum | solution.py:119
  299.3 44.3 %reduce-scatter.6.cloned.1.call-done = f32[16,4,8,128]{3,0,2,1:T(8,128)} async-done(((f32[256,4,8,128]{3,0,2,1:T(8,128)}), f32[16,4,8,128]{3,0,2,1:T(8,128)}) %reduce-scatter.6.cloned.1.call-update) | async-done | bytes 262160 | tf_op jit(solution)/shard_map/reduce_scatter | solution.py:143
  345.2 7.1 %collective-permute-done = bf16[16,4096]{1,0:T(8,128)(2,1)S(1)} collective-permute-done((bf16[16,4096]{1,0:T(8,128)(2,1)S(1)}, bf16[16,4096]{1,0:T(8,128)(2,1)S(1)}, u32[]{:S(2)}, u32[]{:S(2)}) %collective-permute-start) | collective-permute-done | bytes 131104 | tf_op jit(solution)/shard_map/ppermute | solution.py:163
  352.2 7.1 %collective-permute-done.1 = bf16[16,4096]{1,0:T(8,128)(2,1)S(1)} collective-permute-done((bf16[16,4096]{1,0:T(8,128)(2,1)S(1)}, bf16[16,4096]{1,0:T(8,128)(2,1)S(1)}, u32[]{:S(2)}, u32[]{:S(2)}) %collective-permute-start.1) | collective-permute-done | bytes 131104 | tf_op jit(solution)/shard_map/ppermute | solution.py:163
  359.3 7.1 %collective-permute-done.2 = bf16[16,4096]{1,0:T(8,128)(2,1)S(1)} collective-permute-done((bf16[16,4096]{1,0:T(8,128)(2,1)S(1)}, bf16[16,4096]{1,0:T(8,128)(2,1)S(1)}, u32[]{:S(2)}, u32[]{:S(2)}) %collective-permute-start.2) | collective-permute-done | bytes 131104 | tf_op jit(solution)/shard_map/ppermute | solution.py:163
  366.4 7.1 %collective-permute-done.3 = bf16[16,4096]{1,0:T(8,128)(2,1)S(1)} collective-permute-done((bf16[16,4096]{1,0:T(8,128)(2,1)S(1)}, bf16[16,4096]{1,0:T(8,128)(2,1)S(1)}, u32[]{:S(2)}, u32[]{:S(2)}) %collective-permute-start.3) | collective-permute-done | bytes 131104 | tf_op jit(solution)/shard_map/ppermute | solution.py:163
  373.5 7.1 %collective-permute-done.4 = bf16[16,4096]{1,0:T(8,128)(2,1)S(1)} collective-permute-done((bf16[16,4096]{1,0:T(8,128)(2,1)S(1)}, bf16[16,4096]{1,0:T(8,128)(2,1)S(1)}, u32[]{:S(2)}, u32[]{:S(2)}) %collective-permute-start.4) | collective-permute-done | bytes 131104 | tf_op jit(solution)/shard_map/ppermute | solution.py:163
  380.6 7.1 %collective-permute-done.5 = bf16[16,4096]{1,0:T(8,128)(2,1)S(1)} collective-permute-done((bf16[16,4096]{1,0:T(8,128)(2,1)S(1)}, bf16[16,4096]{1,0:T(8,128)(2,1)S(1)}, u32[]{:S(2)}, u32[]{:S(2)}) %collective-permute-start.5) | collective-permute-done | bytes 131104 | tf_op jit(solution)/shard_map/ppermute | solution.py:163
  387.7 7.1 %collective-permute-done.6 = bf16[16,4096]{1,0:T(8,128)(2,1)S(1)} collective-permute-done((bf16[16,4096]{1,0:T(8,128)(2,1)S(1)}, bf16[16,4096]{1,0:T(8,128)(2,1)S(1)}, u32[]{:S(2)}, u32[]{:S(2)}) %collective-permute-start.6) | collective-permute-done | bytes 131104 | tf_op jit(solution)/shard_map/ppermute | solution.py:163
  394.8 7.1 %collective-permute-done.7 = bf16[16,4096]{1,0:T(8,128)(2,1)S(1)} collective-permute-done((bf16[16,4096]{1,0:T(8,128)(2,1)S(1)}, bf16[16,4096]{1,0:T(8,128)(2,1)S(1)}, u32[]{:S(2)}, u32[]{:S(2)}) %collective-permute-start.7) | collective-permute-done | bytes 131104 | tf_op jit(solution)/shard_map/ppermute | solution.py:163
  401.9 7.1 %collective-permute-done.8 = bf16[16,4096]{1,0:T(8,128)(2,1)S(1)} collective-permute-done((bf16[16,4096]{1,0:T(8,128)(2,1)S(1)}, bf16[16,4096]{1,0:T(8,128)(2,1)S(1)}, u32[]{:S(2)}, u32[]{:S(2)}) %collective-permute-start.8) | collective-permute-done | bytes 131104 | tf_op jit(solution)/shard_map/ppermute | solution.py:163
  409.0 7.1 %collective-permute-done.9 = bf16[16,4096]{1,0:T(8,128)(2,1)S(1)} collective-permute-done((bf16[16,4096]{1,0:T(8,128)(2,1)S(1)}, bf16[16,4096]{1,0:T(8,128)(2,1)S(1)}, u32[]{:S(2)}, u32[]{:S(2)}) %collective-permute-start.9) | collective-permute-done | bytes 131104 | tf_op jit(solution)/shard_map/ppermute | solution.py:163
  416.1 7.1 %collective-permute-done.10 = bf16[16,4096]{1,0:T(8,128)(2,1)S(1)} collective-permute-done((bf16[16,4096]{1,0:T(8,128)(2,1)S(1)}, bf16[16,4096]{1,0:T(8,128)(2,1)S(1)}, u32[]{:S(2)}, u32[]{:S(2)}) %collective-permute-start.10) | collective-permute-done | bytes 131104 | tf_op jit(solution)/shard_map/ppermute | solution.py:163
  423.1 7.1 %collective-permute-done.11 = bf16[16,4096]{1,0:T(8,128)(2,1)S(1)} collective-permute-done((bf16[16,4096]{1,0:T(8,128)(2,1)S(1)}, bf16[16,4096]{1,0:T(8,128)(2,1)S(1)}, u32[]{:S(2)}, u32[]{:S(2)}) %collective-permute-start.11) | collective-permute-done | bytes 131104 | tf_op jit(solution)/shard_map/ppermute | solution.py:163
  430.2 7.1 %collective-permute-done.12 = bf16[16,4096]{1,0:T(8,128)(2,1)S(1)} collective-permute-done((bf16[16,4096]{1,0:T(8,128)(2,1)S(1)}, bf16[16,4096]{1,0:T(8,128)(2,1)S(1)}, u32[]{:S(2)}, u32[]{:S(2)}) %collective-permute-start.12) | collective-permute-done | bytes 131104 | tf_op jit(solution)/shard_map/ppermute | solution.py:163
  437.3 7.1 %collective-permute-done.13 = bf16[16,4096]{1,0:T(8,128)(2,1)S(1)} collective-permute-done((bf16[16,4096]{1,0:T(8,128)(2,1)S(1)}, bf16[16,4096]{1,0:T(8,128)(2,1)S(1)}, u32[]{:S(2)}, u32[]{:S(2)}) %collective-permute-start.13) | collective-permute-done | bytes 131104 | tf_op jit(solution)/shard_map/ppermute | solution.py:163
  444.4 7.1 %collective-permute-done.14 = bf16[16,4096]{1,0:T(8,128)(2,1)S(1)} collective-permute-done((bf16[16,4096]{1,0:T(8,128)(2,1)S(1)}, bf16[16,4096]{1,0:T(8,128)(2,1)S(1)}, u32[]{:S(2)}, u32[]{:S(2)}) %collective-permute-start.14) | collective-permute-done | bytes 131104 | tf_op jit(solution)/shard_map/ppermute | solution.py:163
  452.2 2.1 fusion.16
  454.3 12.0 %reduce-scatter.8.cloned.1.call-done = f32[256,256]{1,0:T(8,128)} async-done(((f32[256,512]{1,0:T(8,128)}), f32[256,256]{1,0:T(8,128)}) %reduce-scatter.8.cloned.1.call-update) | async-done | bytes 262160 | tf_op jit(solution)/shard_map/reduce_scatter | solution.py:168
  466.3 1.6 convert_element_type.65
  (150 shorter events, 25.4 us)
Async XLA Ops:
  6.5 129.3 %all-reduce.4.cloned.1.call-start = ((), (), s32[]{:S(2)}) async-start(), calls=%async_computation.6 | async-start | bytes 9437184 | tf_op jit(solution)/shard_map/psum | solution.py:119
  16.1 6.3 %copy-start.21 = (s32[2,128]{1,0:T(2,128)S(1)}, s32[2,128]{1,0:T(2,128)}, u32[]{:S(2)}) copy-start(s32[2,128]{1,0:T(2,128)} %param.16) | copy-start | bytes 3076
  16.1 282.4 %reduce-scatter.10.cloned.1.call-start = ((), (), s32[]{:S(2)}) async-start(), calls=%async_computation.5 | async-start | bytes 139264
  22.3 120.3 %copy-start.19 = (pred[512]{0:T(512)(128)(4,1)}, pred[512]{0:T(512)(128)(4,1)S(1)}, u32[]{:S(2)}) copy-start(pred[512]{0:T(512)(128)(4,1)S(1)} %get-tuple-element.92) | copy-start | bytes 1540
  149.6 63.9 %copy-start.10 = (f32[128,4,8]{0,2,1:T(8,128)}, f32[128,4,8]{0,2,1:T(8,128)S(1)}, u32[]{:S(2)}) copy-start(f32[128,4,8]{0,2,1:T(8,128)S(1)} %broadcast_maximum_fusion.1) | copy-start | bytes 49156
  149.6 63.8 %copy-start.15 = (f32[128,4,8]{0,2,1:T(8,128)S(1)}, f32[128,4,8]{0,2,1:T(8,128)}, u32[]{:S(2)}) copy-start(f32[128,4,8]{0,2,1:T(8,128)} %get-tuple-element.78) | copy-start | bytes 49156
  149.6 65.5 %copy-start.9 = (bf16[1,512,512]{1,2,0:T(8,128)(2,1)S(1)}, bf16[1,512,512]{1,2,0:T(8,128)(2,1)}, u32[]{:S(2)}) copy-start(bf16[1,512,512]{1,2,0:T(8,128)(2,1)} %copy.74) | copy-start | bytes 1572868
  214.8 128.8 %reduce-scatter.6.cloned.1.call-start = ((), (), s32[]{:S(2)}) async-start(), calls=%async_computation.3 | async-start | bytes 4456448 | tf_op jit(solution)/shard_map/reduce_scatter | solution.py:143
  215.1 5.8 %copy-start.8 = (bf16[1,512,512]{1,2,0:T(8,128)(2,1)S(1)}, bf16[1,512,512]{1,2,0:T(8,128)(2,1)}, u32[]{:S(2)}) copy-start(bf16[1,512,512]{1,2,0:T(8,128)(2,1)} %copy.72) | copy-start | bytes 1572868
  215.1 5.8 %copy-start.11 = (f32[128,4,8]{0,2,1:T(8,128)S(1)}, f32[128,4,8]{0,2,1:T(8,128)}, u32[]{:S(2)}) copy-start(f32[128,4,8]{0,2,1:T(8,128)} %copy-done.10) | copy-start | bytes 49156
  215.1 5.8 %copy-start.16 = (f32[128,4,8]{0,2,1:T(8,128)S(1)}, f32[128,4,8]{0,2,1:T(8,128)}, u32[]{:S(2)}) copy-start(f32[128,4,8]{0,2,1:T(8,128)} %get-tuple-element.77) | copy-start | bytes 49156
  215.1 5.8 %copy-start.18 = (pred[512]{0:T(512)(128)(4,1)S(1)}, pred[512]{0:T(512)(128)(4,1)}, u32[]{:S(2)}) copy-start(pred[512]{0:T(512)(128)(4,1)} %get-tuple-element.93) | copy-start | bytes 1540
  220.9 5.5 %copy-start.14 = (f32[256,4,8]{0,2,1:T(8,128)S(1)}, f32[256,4,8]{0,2,1:T(8,128)}, u32[]{:S(2)}) copy-start(f32[256,4,8]{0,2,1:T(8,128)} %get-tuple-element.54) | copy-start | bytes 98308
  229.0 68.5 %copy-start.5 = (f32[256,4,128]{2,0,1:T(8,128)S(1)}, f32[256,4,128]{2,0,1:T(8,128)}, u32[]{:S(2)}) copy-start(f32[256,4,128]{2,0,1:T(8,128)} %get-tuple-element.39) | copy-start | bytes 1572868
  229.0 237.3 %reduce-scatter.8.cloned.1.call-start = ((), (), s32[]{:S(2)}) async-start(), calls=%async_computation.4 | async-start | bytes 786432 | tf_op jit(solution)/shard_map/reduce_scatter | solution.py:168
  345.1 7.1 %collective-permute-start = (bf16[16,4096]{1,0:T(8,128)(2,1)S(1)}, bf16[16,4096]{1,0:T(8,128)(2,1)S(1)}, u32[]{:S(2)}, u32[]{:S(2)}) collective-permute-start(bf16[16,4096]{1,0:T(8,128)(2,1)S(1)} %bitcast.149), channel_id=1, source_target_pairs={{0,2},{2,4},{4,6},{6,8},{8,10},{10,12},{12,14},{14,16},{16,18},{18... | collective-permute-start | bytes 393224 | tf_op jit(solution)/shard_map/ppermute | solution.py:163
  352.2 7.1 %collective-permute-start.1 = (bf16[16,4096]{1,0:T(8,128)(2,1)S(1)}, bf16[16,4096]{1,0:T(8,128)(2,1)S(1)}, u32[]{:S(2)}, u32[]{:S(2)}) collective-permute-start(bf16[16,4096]{1,0:T(8,128)(2,1)S(1)} %collective-permute-done), channel_id=1, source_target_pairs={{0,2},{2,4},{4,6},{6,8},{8,10},{10,12},{12,14},{14,16},{16,18},{18... | collective-permute-start | bytes 393224 | tf_op jit(solution)/shard_map/ppermute | solution.py:163
  359.3 7.1 %collective-permute-start.2 = (bf16[16,4096]{1,0:T(8,128)(2,1)S(1)}, bf16[16,4096]{1,0:T(8,128)(2,1)S(1)}, u32[]{:S(2)}, u32[]{:S(2)}) collective-permute-start(bf16[16,4096]{1,0:T(8,128)(2,1)S(1)} %collective-permute-done.1), channel_id=1, source_target_pairs={{0,2},{2,4},{4,6},{6,8},{8,10},{10,12},{12,14},{14,16},{16,18},{18... | collective-permute-start | bytes 393224 | tf_op jit(solution)/shard_map/ppermute | solution.py:163
  366.4 7.1 %collective-permute-start.3 = (bf16[16,4096]{1,0:T(8,128)(2,1)S(1)}, bf16[16,4096]{1,0:T(8,128)(2,1)S(1)}, u32[]{:S(2)}, u32[]{:S(2)}) collective-permute-start(bf16[16,4096]{1,0:T(8,128)(2,1)S(1)} %collective-permute-done.2), channel_id=1, source_target_pairs={{0,2},{2,4},{4,6},{6,8},{8,10},{10,12},{12,14},{14,16},{16,18},{18... | collective-permute-start | bytes 393224 | tf_op jit(solution)/shard_map/ppermute | solution.py:163
  373.5 7.1 %collective-permute-start.4 = (bf16[16,4096]{1,0:T(8,128)(2,1)S(1)}, bf16[16,4096]{1,0:T(8,128)(2,1)S(1)}, u32[]{:S(2)}, u32[]{:S(2)}) collective-permute-start(bf16[16,4096]{1,0:T(8,128)(2,1)S(1)} %collective-permute-done.3), channel_id=1, source_target_pairs={{0,2},{2,4},{4,6},{6,8},{8,10},{10,12},{12,14},{14,16},{16,18},{18... | collective-permute-start | bytes 393224 | tf_op jit(solution)/shard_map/ppermute | solution.py:163
  380.6 7.1 %collective-permute-start.5 = (bf16[16,4096]{1,0:T(8,128)(2,1)S(1)}, bf16[16,4096]{1,0:T(8,128)(2,1)S(1)}, u32[]{:S(2)}, u32[]{:S(2)}) collective-permute-start(bf16[16,4096]{1,0:T(8,128)(2,1)S(1)} %collective-permute-done.4), channel_id=1, source_target_pairs={{0,2},{2,4},{4,6},{6,8},{8,10},{10,12},{12,14},{14,16},{16,18},{18... | collective-permute-start | bytes 393224 | tf_op jit(solution)/shard_map/ppermute | solution.py:163
  387.7 7.1 %collective-permute-start.6 = (bf16[16,4096]{1,0:T(8,128)(2,1)S(1)}, bf16[16,4096]{1,0:T(8,128)(2,1)S(1)}, u32[]{:S(2)}, u32[]{:S(2)}) collective-permute-start(bf16[16,4096]{1,0:T(8,128)(2,1)S(1)} %collective-permute-done.5), channel_id=1, source_target_pairs={{0,2},{2,4},{4,6},{6,8},{8,10},{10,12},{12,14},{14,16},{16,18},{18... | collective-permute-start | bytes 393224 | tf_op jit(solution)/shard_map/ppermute | solution.py:163
  394.8 7.1 %collective-permute-start.7 = (bf16[16,4096]{1,0:T(8,128)(2,1)S(1)}, bf16[16,4096]{1,0:T(8,128)(2,1)S(1)}, u32[]{:S(2)}, u32[]{:S(2)}) collective-permute-start(bf16[16,4096]{1,0:T(8,128)(2,1)S(1)} %collective-permute-done.6), channel_id=1, source_target_pairs={{0,2},{2,4},{4,6},{6,8},{8,10},{10,12},{12,14},{14,16},{16,18},{18... | collective-permute-start | bytes 393224 | tf_op jit(solution)/shard_map/ppermute | solution.py:163
  401.9 7.1 %collective-permute-start.8 = (bf16[16,4096]{1,0:T(8,128)(2,1)S(1)}, bf16[16,4096]{1,0:T(8,128)(2,1)S(1)}, u32[]{:S(2)}, u32[]{:S(2)}) collective-permute-start(bf16[16,4096]{1,0:T(8,128)(2,1)S(1)} %collective-permute-done.7), channel_id=1, source_target_pairs={{0,2},{2,4},{4,6},{6,8},{8,10},{10,12},{12,14},{14,16},{16,18},{18... | collective-permute-start | bytes 393224 | tf_op jit(solution)/shard_map/ppermute | solution.py:163
  409.0 7.1 %collective-permute-start.9 = (bf16[16,4096]{1,0:T(8,128)(2,1)S(1)}, bf16[16,4096]{1,0:T(8,128)(2,1)S(1)}, u32[]{:S(2)}, u32[]{:S(2)}) collective-permute-start(bf16[16,4096]{1,0:T(8,128)(2,1)S(1)} %collective-permute-done.8), channel_id=1, source_target_pairs={{0,2},{2,4},{4,6},{6,8},{8,10},{10,12},{12,14},{14,16},{16,18},{18... | collective-permute-start | bytes 393224 | tf_op jit(solution)/shard_map/ppermute | solution.py:163
  416.0 7.1 %collective-permute-start.10 = (bf16[16,4096]{1,0:T(8,128)(2,1)S(1)}, bf16[16,4096]{1,0:T(8,128)(2,1)S(1)}, u32[]{:S(2)}, u32[]{:S(2)}) collective-permute-start(bf16[16,4096]{1,0:T(8,128)(2,1)S(1)} %collective-permute-done.9), channel_id=1, source_target_pairs={{0,2},{2,4},{4,6},{6,8},{8,10},{10,12},{12,14},{14,16},{16,18},{18... | collective-permute-start | bytes 393224 | tf_op jit(solution)/shard_map/ppermute | solution.py:163
  423.1 7.1 %collective-permute-start.11 = (bf16[16,4096]{1,0:T(8,128)(2,1)S(1)}, bf16[16,4096]{1,0:T(8,128)(2,1)S(1)}, u32[]{:S(2)}, u32[]{:S(2)}) collective-permute-start(bf16[16,4096]{1,0:T(8,128)(2,1)S(1)} %collective-permute-done.10), channel_id=1, source_target_pairs={{0,2},{2,4},{4,6},{6,8},{8,10},{10,12},{12,14},{14,16},{16,18},{18... | collective-permute-start | bytes 393224 | tf_op jit(solution)/shard_map/ppermute | solution.py:163
  430.2 7.1 %collective-permute-start.12 = (bf16[16,4096]{1,0:T(8,128)(2,1)S(1)}, bf16[16,4096]{1,0:T(8,128)(2,1)S(1)}, u32[]{:S(2)}, u32[]{:S(2)}) collective-permute-start(bf16[16,4096]{1,0:T(8,128)(2,1)S(1)} %collective-permute-done.11), channel_id=1, source_target_pairs={{0,2},{2,4},{4,6},{6,8},{8,10},{10,12},{12,14},{14,16},{16,18},{18... | collective-permute-start | bytes 393224 | tf_op jit(solution)/shard_map/ppermute | solution.py:163
  437.3 7.1 %collective-permute-start.13 = (bf16[16,4096]{1,0:T(8,128)(2,1)S(1)}, bf16[16,4096]{1,0:T(8,128)(2,1)S(1)}, u32[]{:S(2)}, u32[]{:S(2)}) collective-permute-start(bf16[16,4096]{1,0:T(8,128)(2,1)S(1)} %collective-permute-done.12), channel_id=1, source_target_pairs={{0,2},{2,4},{4,6},{6,8},{8,10},{10,12},{12,14},{14,16},{16,18},{18... | collective-permute-start | bytes 393224 | tf_op jit(solution)/shard_map/ppermute | solution.py:163
  444.4 7.1 %collective-permute-start.14 = (bf16[16,4096]{1,0:T(8,128)(2,1)S(1)}, bf16[16,4096]{1,0:T(8,128)(2,1)S(1)}, u32[]{:S(2)}, u32[]{:S(2)}) collective-permute-start(bf16[16,4096]{1,0:T(8,128)(2,1)S(1)} %collective-permute-done.13), channel_id=1, source_target_pairs={{0,2},{2,4},{4,6},{6,8},{8,10},{10,12},{12,14},{14,16},{16,18},{18... | collective-permute-start | bytes 393224 | tf_op jit(solution)/shard_map/ppermute | solution.py:163
  444.4 7.8 %copy-start.22 = (bf16[4096,512]{1,0:T(8,128)(2,1)S(1)}, bf16[4096,512]{1,0:T(8,128)(2,1)}, u32[]{:S(2)}) copy-start(bf16[4096,512]{1,0:T(8,128)(2,1)} %param.13) | copy-start | bytes 12582916
  452.1 15.8 %copy-start.1 = (bf16[512,512]{1,0:T(8,128)(2,1)S(1)}, bf16[512,512]{1,0:T(8,128)(2,1)}, u32[]{:S(2)}) copy-start(bf16[512,512]{1,0:T(8,128)(2,1)} %param.11) | copy-start | bytes 1572868
  (10 other events, 22.1 us)
Sparse Core Ops, SparseCore 0:
  16.2 119.6 all-reduce.3
  214.9 52.9 reduce-scatter.9
  271.8 71.8 reduce-scatter.5
  454.4 11.8 reduce-scatter.7
